TPU v7x, 32 devices: a whole 2x2x4 slice. The times are simulated.
32 devices in a mesh: rep: 16 (over z, y, core), grp: 2 (over x).
Axes of the slice: x: 2, y: 2, z: 4, core: 2. Of those that a mesh axis runs over, the one named last changes fastest.
Arguments:
- tokens: bfloat16 [4096, 1024], P(('rep', 'grp')), may hold values from -6 to 6
- cotangent: float32 [4096, 1024], P(('rep', 'grp')), may hold values from -6 to 6
- expert_index: int32 [4096, 8], P(('rep', 'grp')), may hold values from 0 to 31, as said below
- gate_weight: float32 [4096, 8], P(('rep', 'grp')), may hold values from 0.1 to 1
- attn_params: float32 [3147776], P(('rep', 'grp')), may hold values from -10 to 10
- attn_first: float32 [3147776], P(('rep', 'grp')), may hold values from -15 to 15
- attn_second: float32 [3147776], P(('rep', 'grp')), may hold values from 1 to 400
- expert_params: float32 [1572864], P(('rep', 'grp')), may hold values from -8 to 8
- expert_first: float32 [1572864], P(('rep', 'grp')), may hold values from -15 to 15
- expert_second: float32 [1572864], P(('rep', 'grp')), may hold values from 1 to 400
Outputs:
- output: float32 [4096, 1024], P(('rep', 'grp'))
- grad_tokens: float32 [4096, 1024], P(('rep', 'grp'))
- attn_grad: float32 [3147776], P(('rep', 'grp'))
- expert_grad: float32 [1572864], P(('rep', 'grp'))
- new_attn_params: float32 [3147776], P(('rep', 'grp'))
- new_attn_first: float32 [3147776], P(('rep', 'grp'))
- new_attn_second: float32 [3147776], P(('rep', 'grp'))
- new_expert_params: float32 [1572864], P(('rep', 'grp'))
- new_expert_first: float32 [1572864], P(('rep', 'grp'))
- new_expert_second: float32 [1572864], P(('rep', 'grp'))
Inputs may be any that keep to these rules, and one draw needn't show every extreme that they name: `expert_index`: each row names 8 different experts. Among the 128 rows of one device, each expert below 1 is named by 8 to 32 rows, and in every draw one device has exactly 32 rows naming one of them.
All inputs are finite; a program needn't handle non-finite values.
Results may differ from a plain program's by a relative error of at most 0.012.
Values may be sent and summed in bfloat16 or wider, within the bound.
No kernel may reach another device: no remote copies, remote signals or barrier semaphores. Data moves between devices by JAX's collectives and lax.ppermute only.
A program may use at most 128 MiB of HBM per device.

v0:
```python
import jax
import jax.numpy as jnp
from jax import lax
from jax.sharding import PartitionSpec as P

MODEL_WIDTH = 1024
QUERY_HEADS = 16
KEY_VALUE_HEADS = 8
HEAD_SIZE = 64
FF = 512
EXP_WIN = 1
STEP = 5
PROJ = 2048
CAP = 32
NORM_EPS = 1e-06
ROPE_BASE = 10000.0
ATTN_MULT = 0.015625
RESID_MULT = 0.22
LEARN_RATE = 0.05
BETA_ONE = 0.9
BETA_TWO = 0.95
ADAM_EPS = 1e-08
DECAY = 0.1


def unpack_attention(flat_vec):
    start_qkv = 2 * MODEL_WIDTH
    start_out = 2 * MODEL_WIDTH + MODEL_WIDTH * PROJ
    return (
        flat_vec[:MODEL_WIDTH],
        flat_vec[MODEL_WIDTH:start_qkv],
        flat_vec[start_qkv:start_out].reshape(MODEL_WIDTH, PROJ),
        flat_vec[start_out:].reshape(QUERY_HEADS * HEAD_SIZE, MODEL_WIDTH),
    )


def unpack_experts(flat_vec):
    split_at = EXP_WIN * MODEL_WIDTH * 2 * FF
    return (
        flat_vec[:split_at].reshape(EXP_WIN, MODEL_WIDTH, 2 * FF),
        flat_vec[split_at:].reshape(EXP_WIN, FF, MODEL_WIDTH),
    )


def rope_tables(sequence_length):
    half_width = HEAD_SIZE // 2
    frequency = ROPE_BASE ** (-(jnp.arange(half_width).astype(jnp.float32) * 2.0) / HEAD_SIZE)
    angles = jnp.arange(sequence_length).astype(jnp.float32)[:, None] * frequency[None, :]
    cos_table = jnp.concatenate([jnp.cos(angles), jnp.cos(angles)], axis=1)
    sin_table = jnp.concatenate([jnp.sin(angles), jnp.sin(angles)], axis=1)
    return (cos_table[:, None, :], sin_table[:, None, :])


def rotate_half(values):
    half_width = values.shape[-1] // 2
    return jnp.concatenate([-values[..., half_width:], values[..., :half_width]], axis=-1)


def apply_rope(values, cos_table, sin_table):
    return values * cos_table + rotate_half(values) * sin_table


def undo_rope(grads_in, cos_table, sin_table):
    return grads_in * cos_table - rotate_half(grads_in * sin_table)


def rms_forward(values, gain_vec):
    inv_rms = lax.rsqrt(jnp.mean(values * values, axis=-1, keepdims=True) + NORM_EPS)
    return (values * inv_rms * gain_vec, inv_rms)


def rms_backward(values, inv_rms, gain_vec, grad_normed):
    weighted = grad_normed * gain_vec
    grad_values = inv_rms * weighted - values * (inv_rms * inv_rms * inv_rms) * jnp.mean(
        weighted * values, axis=-1, keepdims=True
    )
    grad_gain = jnp.sum(grad_normed * values * inv_rms, axis=0)
    return (grad_values, grad_gain)


def route_tables(index_rows, gate_rows):
    experts_here = jnp.arange(EXP_WIN)
    matches = index_rows[:, :, None] == experts_here[None, None, :]
    member = jnp.any(matches, axis=1)
    weight = jnp.sum(jnp.where(matches, gate_rows[:, :, None], 0.0), axis=1)
    position = jnp.cumsum(member.astype(jnp.int32), axis=0) - 1
    slot_index = jnp.where(member, position, CAP)
    dispatch = jnp.transpose(slot_index)[:, None, :] == jnp.arange(CAP)[None, :, None]
    return (member, weight, slot_index, dispatch)


def causal_scores(rotated_query, keys_rot):
    sequence_length = rotated_query.shape[0]
    scores = (
        jnp.einsum("tgd,sd->gts", rotated_query, keys_rot, preferred_element_type=jnp.float32)
        * ATTN_MULT
    )
    causal = lax.broadcasted_iota(
        jnp.int32, (sequence_length, sequence_length), 0
    ) >= lax.broadcasted_iota(jnp.int32, (sequence_length, sequence_length), 1)
    return jnp.where(causal[None], scores, -jnp.inf)


def head_forward(pieces):
    rotated_query, keys_rot, value_low = pieces
    scores = causal_scores(rotated_query, keys_rot)
    top_score = jnp.max(scores, axis=-1, keepdims=True)
    log_total = top_score + jnp.log(jnp.sum(jnp.exp(scores - top_score), axis=-1, keepdims=True))
    probs_low = jnp.exp(scores - log_total).astype(jnp.bfloat16)
    attention_output = jnp.einsum(
        "gts,sd->tgd", probs_low, value_low, preferred_element_type=jnp.float32
    )
    return (attention_output.astype(jnp.bfloat16), log_total)


def head_backward(pieces):
    rotated_query, keys_rot, value_low, attention_output, grad_att, log_total = pieces
    scores = causal_scores(rotated_query, keys_rot)
    prob_f = jnp.exp(scores - log_total)
    probs_low = prob_f.astype(jnp.bfloat16)
    delta = jnp.sum(grad_att.astype(jnp.float32) * attention_output.astype(jnp.float32), axis=-1)
    grad_probs = jnp.einsum("tgd,sd->gts", grad_att, value_low, preferred_element_type=jnp.float32)
    grad_scores = (prob_f * (grad_probs - jnp.transpose(delta)[:, :, None]) * ATTN_MULT).astype(
        jnp.bfloat16
    )
    value_gradient = jnp.einsum(
        "gts,tgd->sd", probs_low, grad_att, preferred_element_type=jnp.float32
    )
    query_gradient = jnp.einsum(
        "gts,sd->tgd", grad_scores, keys_rot, preferred_element_type=jnp.float32
    )
    key_gradient = jnp.einsum(
        "gts,tgd->sd", grad_scores, rotated_query, preferred_element_type=jnp.float32
    )
    return (query_gradient, key_gradient, value_gradient)


def adamw(current, gradient, moment_one, moment_two):
    moment_one_new = BETA_ONE * moment_one + (1.0 - BETA_ONE) * gradient
    moment_two_new = BETA_TWO * moment_two + (1.0 - BETA_TWO) * gradient * gradient
    first_hat = moment_one_new / (1.0 - BETA_ONE**STEP)
    second_hat = moment_two_new / (1.0 - BETA_TWO**STEP)
    updated = current - LEARN_RATE * (
        first_hat / (jnp.sqrt(second_hat) + ADAM_EPS) + DECAY * current
    )
    return (updated, moment_one_new, moment_two_new)


def per_device(
    tokens,
    cotangent,
    expert_index,
    gate_weight,
    attn_params,
    attn_first,
    attn_second,
    expert_params,
    expert_first,
    expert_second,
):
    single_float = jnp.float32
    rep_count = lax.axis_size("rep")
    grp_count = lax.axis_size("grp")
    attn_low = attn_params.astype(jnp.bfloat16)
    expert_low = expert_params.astype(jnp.bfloat16)
    attn_cube = attn_low.reshape(1, 1, attn_low.shape[0])
    expert_cube = expert_low.reshape(1, 1, expert_low.shape[0])
    attn_part, expert_part = (
        lax.all_gather(attn_cube, "rep", axis=0, tiled=True),
        lax.all_gather(expert_cube, "rep", axis=0, tiled=True),
    )
    attn_whole, expert_whole = (
        lax.all_gather(attn_part, "grp", axis=1, tiled=True),
        lax.all_gather(expert_part, "grp", axis=1, tiled=True),
    )
    attn_full = attn_whole.reshape(-1)
    expert_full = expert_whole.reshape(-1)
    gain_one, gain_two, w_qkv, w_out = unpack_attention(attn_full)
    w_gate_up, w_down = unpack_experts(expert_full)
    sequence_length = tokens.shape[0]
    heads_per_group = QUERY_HEADS // KEY_VALUE_HEADS
    gain_one_f = gain_one.astype(single_float)
    gain_two_f = gain_two.astype(single_float)
    inputs = tokens.astype(single_float)
    normed_one, scale_one = rms_forward(inputs, gain_one_f)
    normed_one = normed_one.astype(jnp.bfloat16)
    query_key_value = jnp.dot(normed_one, w_qkv, preferred_element_type=single_float)
    query = query_key_value[:, : QUERY_HEADS * HEAD_SIZE].reshape(
        sequence_length, QUERY_HEADS, HEAD_SIZE
    )
    unrotated_keys = query_key_value[
        :, QUERY_HEADS * HEAD_SIZE : (QUERY_HEADS + KEY_VALUE_HEADS) * HEAD_SIZE
    ].reshape(sequence_length, KEY_VALUE_HEADS, HEAD_SIZE)
    projected_value = query_key_value[:, (QUERY_HEADS + KEY_VALUE_HEADS) * HEAD_SIZE :].reshape(
        sequence_length, KEY_VALUE_HEADS, HEAD_SIZE
    )
    cos_table, sin_table = rope_tables(sequence_length)
    rotated_query = apply_rope(query, cos_table, sin_table).astype(jnp.bfloat16)
    keys_rot = apply_rope(unrotated_keys, cos_table, sin_table).astype(jnp.bfloat16)
    value_low = projected_value.astype(jnp.bfloat16)
    query_per_head = jnp.transpose(
        rotated_query.reshape(sequence_length, KEY_VALUE_HEADS, heads_per_group, HEAD_SIZE),
        (1, 0, 2, 3),
    )
    keys_heads = jnp.transpose(keys_rot, (1, 0, 2))
    value_heads = jnp.transpose(value_low, (1, 0, 2))
    attended_heads, log_totals = lax.map(head_forward, (query_per_head, keys_heads, value_heads))
    attention_output = jnp.transpose(attended_heads, (1, 0, 2, 3)).reshape(
        sequence_length, QUERY_HEADS * HEAD_SIZE
    )
    hidden = inputs + RESID_MULT * jnp.dot(
        attention_output, w_out, preferred_element_type=single_float
    )
    normed_two, scale_two = rms_forward(hidden, gain_two_f)
    normed_two = normed_two.astype(jnp.bfloat16)
    member, weight, slot_index, dispatch = route_tables(expert_index, gate_weight)
    blocks = jnp.einsum(
        "ect,td->ecd",
        dispatch.astype(jnp.bfloat16),
        normed_two,
        preferred_element_type=single_float,
    ).astype(jnp.bfloat16)
    gate_up = jnp.einsum("ecd,edf->ecf", blocks, w_gate_up, preferred_element_type=single_float)
    gate_part = gate_up[..., :FF]
    up_part = gate_up[..., FF:]
    sigma = jax.nn.sigmoid(gate_part)
    activated = (gate_part * sigma * up_part).astype(jnp.bfloat16)
    expert_out = jnp.einsum("ecf,efd->ecd", activated, w_down, preferred_element_type=single_float)
    clipped = jnp.minimum(slot_index, CAP - 1)
    expert = 0
    mixture = weight * jnp.take(expert_out[expert], clipped[:, expert], axis=0)
    output = hidden + RESID_MULT * mixture
    grad_mix = RESID_MULT * cotangent
    scaled = jnp.transpose(weight)[:, :, None] * grad_mix[None, :, :]
    grad_blocks = jnp.einsum(
        "ect,etd->ecd", dispatch.astype(single_float), scaled, precision=lax.Precision.HIGHEST
    ).astype(jnp.bfloat16)
    grad_w_down = jnp.einsum(
        "ecf,ecd->efd", activated, grad_blocks, preferred_element_type=single_float
    )
    grad_act = jnp.einsum("ecd,efd->ecf", grad_blocks, w_down, preferred_element_type=single_float)
    silu_slope = sigma * (1.0 + gate_part * (1.0 - sigma))
    grad_gate_up = jnp.concatenate(
        [grad_act * up_part * silu_slope, grad_act * gate_part * sigma], axis=-1
    ).astype(jnp.bfloat16)
    grad_w_gate_up = jnp.einsum(
        "ecd,ecf->edf", blocks, grad_gate_up, preferred_element_type=single_float
    )
    expert_grad_full = jnp.concatenate([grad_w_gate_up.reshape(-1), grad_w_down.reshape(-1)])
    grad_in_blocks = jnp.einsum(
        "ecf,edf->ecd", grad_gate_up, w_gate_up, preferred_element_type=single_float
    )
    expert = 0
    grad_normed_two = member.astype(single_float) * jnp.take(
        grad_in_blocks[expert], clipped[:, expert], axis=0
    )
    grad_hidden_n, grad_gain_two = rms_backward(hidden, scale_two, gain_two_f, grad_normed_two)
    grad_hidden = cotangent + grad_hidden_n
    grad_branch = (RESID_MULT * grad_hidden).astype(jnp.bfloat16)
    grad_w_out = jnp.einsum(
        "ti,tj->ij", attention_output, grad_branch, preferred_element_type=single_float
    )
    attention_output_gradient = jnp.einsum(
        "tj,ij->ti", grad_branch, w_out, preferred_element_type=single_float
    ).astype(jnp.bfloat16)
    attention_gradient_heads = jnp.transpose(
        attention_output_gradient.reshape(
            sequence_length, KEY_VALUE_HEADS, heads_per_group, HEAD_SIZE
        ),
        (1, 0, 2, 3),
    )
    grad_query_h, grad_keys_h, grad_value_h = lax.map(
        head_backward,
        (
            query_per_head,
            keys_heads,
            value_heads,
            attended_heads,
            attention_gradient_heads,
            log_totals,
        ),
    )
    query_gradient = jnp.transpose(grad_query_h, (1, 0, 2, 3)).reshape(
        sequence_length, QUERY_HEADS, HEAD_SIZE
    )
    key_gradient = jnp.transpose(grad_keys_h, (1, 0, 2))
    value_gradient = jnp.transpose(grad_value_h, (1, 0, 2))
    query_gradient = undo_rope(query_gradient, cos_table, sin_table)
    key_gradient = undo_rope(key_gradient, cos_table, sin_table)
    query_key_value_gradient = jnp.concatenate(
        [
            query_gradient.reshape(sequence_length, QUERY_HEADS * HEAD_SIZE),
            key_gradient.reshape(sequence_length, KEY_VALUE_HEADS * HEAD_SIZE),
            value_gradient.reshape(sequence_length, KEY_VALUE_HEADS * HEAD_SIZE),
        ],
        axis=1,
    ).astype(jnp.bfloat16)
    grad_w_qkv = jnp.einsum(
        "ti,tj->ij", normed_one, query_key_value_gradient, preferred_element_type=single_float
    )
    grad_normed_one = jnp.einsum(
        "tj,ij->ti", query_key_value_gradient, w_qkv, preferred_element_type=single_float
    )
    grad_inputs_n, grad_gain_one = rms_backward(inputs, scale_one, gain_one_f, grad_normed_one)
    grad_tokens = grad_hidden + grad_inputs_n
    attn_grad_full = jnp.concatenate(
        [grad_gain_one, grad_gain_two, grad_w_qkv.reshape(-1), grad_w_out.reshape(-1)]
    )
    attn_cube = attn_grad_full.reshape(rep_count, grp_count, -1)
    expert_cube = expert_grad_full.reshape(rep_count, grp_count, -1)
    attn_inner, expert_inner = (
        lax.psum_scatter(attn_cube, "grp", scatter_dimension=1, tiled=True),
        lax.psum_scatter(expert_cube, "grp", scatter_dimension=1, tiled=True),
    )
    attn_owned, expert_owned = (
        lax.psum_scatter(attn_inner, "rep", scatter_dimension=0, tiled=True),
        lax.psum_scatter(expert_inner, "rep", scatter_dimension=0, tiled=True),
    )
    attn_grad = attn_owned.reshape(-1)
    expert_grad = expert_owned.reshape(-1)
    new_attn, new_attn_first, new_attn_second = adamw(
        attn_params, attn_grad, attn_first, attn_second
    )
    new_expert, new_expert_first, new_expert_second = adamw(
        expert_params, expert_grad, expert_first, expert_second
    )
    return (
        output,
        grad_tokens,
        attn_grad,
        expert_grad,
        new_attn,
        new_attn_first,
        new_attn_second,
        new_expert,
        new_expert_first,
        new_expert_second,
    )


def solution(mesh):
    in_specs = (
        P(("rep", "grp"), None),
        P(("rep", "grp"), None),
        P(("rep", "grp"), None),
        P(("rep", "grp"), None),
        P(("rep", "grp")),
        P(("rep", "grp")),
        P(("rep", "grp")),
        P(("rep", "grp")),
        P(("rep", "grp")),
        P(("rep", "grp")),
    )
    out_specs = (
        P(("rep", "grp"), None),
        P(("rep", "grp"), None),
        P(("rep", "grp")),
        P(("rep", "grp")),
        P(("rep", "grp")),
        P(("rep", "grp")),
        P(("rep", "grp")),
        P(("rep", "grp")),
        P(("rep", "grp")),
        P(("rep", "grp")),
    )
    return jax.shard_map(
        per_device, mesh=mesh, in_specs=in_specs, out_specs=out_specs, check_vma=False
    )
```

profile of v0, /device:TPU:0, one launch (start us, length us, event | category | flops | bytes accessed | tf_op | source)
XLA Modules:
  0.0 892.8 jit_solution(10353545932153896731)
XLA Ops:
  16.0 37.1 %all-gather.10.cloned.1.call-done = bf16[786432]{0:T(1024)(128)(2,1)} async-done(((bf16[49152]{0:T(1024)(128)(2,1)}), bf16[786432]{0:T(1024)(128)(2,1)}) %all-gather.10.cloned.1.call-update) | async-done | bytes 1572880 | tf_op jit(solution)/shard_map/all_gather | solution.py:170
  53.2 2.7 reshape.382
  56.0 103.6 %all-reduce.7.cloned.1.call-done = bf16[1573888]{0:T(1024)(128)(2,1)} async-done(((bf16[1573888]{0:T(1024)(128)(2,1)}), bf16[1573888]{0:T(1024)(128)(2,1)}) %all-reduce.7.cloned.1.call-update) | async-done | bytes 3147792
  159.7 6.0 reshape.381
  168.9 36.8 %all-gather.8.cloned.1.call-done = bf16[16,2,49152]{2,0,1:T(8,128)(2,1)} async-done(((bf16[16,1,49152]{2,0,1:T(8,128)(2,1)}), bf16[16,2,49152]{2,0,1:T(8,128)(2,1)}) %all-gather.8.cloned.1.call-update) | async-done | bytes 3145744 | tf_op jit(solution)/shard_map/all_gather | solution.py:174
  205.7 5.1 copy.87
  210.8 5.1 slice.87
  216.0 4.6 slice.91
  220.6 67.0 %all-gather.6.cloned.1.call-done = bf16[16,2,98368]{2,0,1:T(8,128)(2,1)} async-done(((bf16[16,1,98368]{2,0,1:T(8,128)(2,1)}), bf16[16,2,98368]{2,0,1:T(8,128)(2,1)}) %all-gather.6.cloned.1.call-update) | async-done | bytes 6295568 | tf_op jit(solution)/shard_map/all_gather | solution.py:173
  287.6 10.3 %copy.79 = bf16[16,2,98368]{2,1,0:T(2,128)(2,1)} copy(bf16[16,2,98368]{2,0,1:T(8,128)(2,1)} %all-gather.6.cloned.1.call-done) | data formatting | bytes 12591104 | tf_op jit(solution)/shard_map/all_gather | solution.py:173
  297.9 8.1 reshape.404
  306.0 10.4 %slice.75 = bf16[1537,2048]{1,0:T(8,128)(2,1)} reshape(bf16[3147776]{0:T(1024)(128)(2,1)} %reshape.404) | data formatting | bytes 12591104 | tf_op jit(solution)/shard_map/slice | solution.py:32
  317.1 3.6 fusion.48
  320.9 10.4 %slice.84 = bf16[3074,1024]{1,0:T(8,128)(2,1)} reshape(bf16[3147776]{0:T(1024)(128)(2,1)} %reshape.404) | data formatting | bytes 12591104 | tf_op jit(solution)/shard_map/slice | solution.py:33
  333.9 25.1 %while.26 = (s32[]{:T(128)}, bf16[8,128,2,64]{1,3,2,0:T(8,128)(2,1)}, f32[8,2,128,1]{2,1,3,0:T(2,128)}, bf16[8,128,64]{1,2,0:T(8,128)(2,1)}, bf16[8,128,64]{1,2,...) while((s32[]{:T(128)}, bf16[8,128,2,64]{1,3,2,0:T(8,128)(2,1)}, f32[8,2,128,1]{2,1,3,0:T(2,128)}, ...), condition=%wide.region_4.5_spmd, body=%wide.region_1.4_spmd.sunk | while | flops 8650498 | bytes 534617 | solution.py:207
  373.3 2.8 convolution_bitcast_fusion.6
  376.3 41.5 %while.27 = (s32[]{:T(128)}, f32[8,128,2,64]{1,3,2,0:T(8,128)S(1)}, f32[8,128,64]{1,2,0:T(8,128)S(1)}, bf16[8,128,64]{1,2,0:T(8,128)(2,1)}, bf16[8,128,64]{1,2,0...) while((s32[]{:T(128)}, f32[8,128,2,64]{1,3,2,0:T(8,128)S(1)}, ...), condition=%wide.region_12.14_spmd, body=%wide.region_10.13_spmd.sunk | while | flops 21315328 | bytes 1009789 | solution.py:272
  418.7 3.9 fusion.80
  426.2 3.0 copy.99
  429.2 5.2 copy.98
  435.9 4.8 pad_maximum_fusion.1
  440.7 9.2 %reshape.361 = f32[16,2,49152]{2,1,0:T(2,128)} reshape(f32[1572864]{0:T(1024)} %pad_maximum_fusion.1) | data formatting | bytes 12582912 | tf_op jit(solution)/shard_map/reshape | solution.py:310
  450.0 9.1 %copy.92 = f32[16,2,49152]{2,0,1:T(8,128)} copy(f32[16,2,49152]{2,1,0:T(2,128)} %reshape.361) | data formatting | bytes 12582912 | tf_op jit(solution)/shard_map/reshape | solution.py:310
  459.2 13.8 %pad_maximum_fusion = f32[3147776]{0:T(1024)} fusion(f32[1048576]{0:T(1024)} %bitcast.220, f32[2097152]{0:T(1024)} %bitcast.218, f32[1024]{0:T(1024)S(1)} %get-tuple-element.103, f32[1024]{0:T(1024)S(1)} %get-tuple-element.105), kind=kLoop, calls=%fused_computation.63 | loop fusion | flops 9443328 | bytes 25182208 | tf_op jit(solution)/shard_map/concatenate | solution.py:306
  473.0 19.2 %reshape.357 = f32[16,2,98368]{2,1,0:T(2,128)} reshape(f32[3147776]{0:T(1024)} %pad_maximum_fusion) | data formatting | bytes 25182208 | tf_op jit(solution)/shard_map/reshape | solution.py:309
  492.1 10.3 %copy.90 = f32[16,2,98368]{2,0,1:T(8,128)} copy(f32[16,2,98368]{2,1,0:T(2,128)} %reshape.357) | data formatting | bytes 25182208 | tf_op jit(solution)/shard_map/reshape | solution.py:309
  502.8 33.6 %reduce-scatter.5.cloned.1.call-done = f32[16,1,49152]{2,0,1:T(8,128)} async-done(((f32[16,2,49152]{2,0,1:T(8,128)}), f32[16,1,49152]{2,0,1:T(8,128)}) %reduce-scatter.5.cloned.1.call-update) | async-done | bytes 3145744 | tf_op jit(solution)/shard_map/reduce_scatter | solution.py:313
  536.4 6.8 copy.93
  543.2 141.0 %reduce-scatter.3.cloned.1.call-done = f32[16,1,98368]{2,0,1:T(8,128)} async-done(((f32[16,2,98368]{2,0,1:T(8,128)}), f32[16,1,98368]{2,0,1:T(8,128)}) %reduce-scatter.3.cloned.1.call-update) | async-done | bytes 6295568 | tf_op jit(solution)/shard_map/reduce_scatter | solution.py:312
  684.2 8.7 copy.91
  694.6 184.7 %all-reduce.9.cloned.1.call-done = (f32[16,1,98368]{2,1,0:T(1,128)}, f32[16,1,49152]{2,1,0:T(1,128)}) async-done(((f32[16,1,98368]{2,1,0:T(1,128)}, f32[16,1,49152]{2,1,0:T(1,128)}), (f32[16,1,98368]{2,1,0:T(1,128)}, f32[16,1,49152]{2,1,0:T(1,128)})) %all-reduce.9.cloned.1.call-update) | async-done | bytes 9441296
  879.3 2.7 dynamic-slice_reduce_fusion
  (283 shorter events, 106.6 us)
Async XLA Ops:
  7.2 46.0 %all-gather.10.cloned.1.call-start = ((), (), s32[]{:S(2)}) async-start(), calls=%async_computation.6 | async-start | bytes 1671168 | tf_op jit(solution)/shard_map/all_gather | solution.py:170
  8.8 150.8 %all-reduce.7.cloned.1.call-start = ((), (), s32[]{:S(2)}) async-start(), calls=%async_computation.7 | async-start | bytes 6295552
  16.0 189.7 %all-gather.8.cloned.1.call-start = ((), (), s32[]{:S(2)}) async-start(), calls=%async_computation.3 | async-start | bytes 4718592 | tf_op jit(solution)/shard_map/all_gather | solution.py:174
  55.9 109.9 %copy-start.42 = (f32[128,8]{0,1:T(8,128)S(1)}, f32[128,8]{0,1:T(8,128)}, u32[]{:S(2)}) copy-start(f32[128,8]{0,1:T(8,128)} %param.19) | copy-start | bytes 12292
  55.9 109.9 %copy-start.43 = (s32[128,8]{0,1:T(8,128)S(1)}, s32[128,8]{0,1:T(8,128)}, u32[]{:S(2)}) copy-start(s32[128,8]{0,1:T(8,128)} %param.18) | copy-start | bytes 12292
  55.9 111.2 %copy-start.5 = (bf16[128,1024]{1,0:T(8,128)(2,1)S(1)}, bf16[128,1024]{1,0:T(8,128)(2,1)}, u32[]{:S(2)}) copy-start(bf16[128,1024]{1,0:T(8,128)(2,1)} %param.16) | copy-start | bytes 786436
  56.0 111.9 %copy-start.6 = (f32[128,1024]{1,0:T(8,128)S(1)}, f32[128,1024]{1,0:T(8,128)}, u32[]{:S(2)}) copy-start(f32[128,1024]{1,0:T(8,128)} %param.17) | copy-start | bytes 1572868
  56.0 231.6 %all-gather.6.cloned.1.call-start = ((), (), s32[]{:S(2)}) async-start(), calls=%async_computation.2 | async-start | bytes 9449472 | tf_op jit(solution)/shard_map/all_gather | solution.py:173
  165.7 370.7 %reduce-scatter.5.cloned.1.call-start = ((), (), s32[]{:S(2)}) async-start(), calls=%async_computation.5 | async-start | bytes 9437184 | tf_op jit(solution)/shard_map/reduce_scatter | solution.py:313
  165.9 50.1 %copy-start.44 = (f32[128]{0:T(128)}, f32[128]{0:T(128)S(1)}, u32[]{:S(2)}) copy-start(f32[128]{0:T(128)S(1)} %get-tuple-element.152) | copy-start | bytes 1540
  166.9 49.0 %copy-start.38 = (s32[128]{0:T(128)}, s32[128]{0:T(128)S(1)}, u32[]{:S(2)}) copy-start(s32[128]{0:T(128)S(1)} %get-tuple-element.151) | copy-start | bytes 1540
  167.1 166.1 %copy-start.12 = (f32[128,64]{0,1:T(8,128)}, f32[128,64]{0,1:T(8,128)S(1)}, u32[]{:S(2)}) copy-start(f32[128,64]{0,1:T(8,128)S(1)} %pad_maximum_fusion.10) | copy-start | bytes 98308
  167.1 166.0 %copy-start.14 = (f32[128,64]{0,1:T(8,128)}, f32[128,64]{0,1:T(8,128)S(1)}, u32[]{:S(2)}) copy-start(f32[128,64]{0,1:T(8,128)S(1)} %pad_maximum_fusion.9) | copy-start | bytes 98308
  167.9 149.3 %copy-start.40 = (f32[128]{0:T(128)}, f32[128]{0:T(128)S(1)}, u32[]{:S(2)}) copy-start(f32[128]{0:T(128)S(1)} %get-tuple-element.176) | copy-start | bytes 1540
  333.9 28.3 %copy-start.39 = (s32[128]{0:T(128)S(1)}, s32[128]{0:T(128)}, u32[]{:S(2)}) copy-start(s32[128]{0:T(128)} %copy-done.38) | copy-start | bytes 1540
  333.9 28.5 %copy-start.2 = (bf16[1536,1024]{1,0:T(8,128)(2,1)S(1)}, bf16[1536,1024]{1,0:T(8,128)(2,1)}, u32[]{:S(2)}) copy-start(bf16[1536,1024]{1,0:T(8,128)(2,1)} %slice.87) | copy-start | bytes 9437188
  359.1 3.9 copy-start.23
  362.2 3.8 copy-start.34
  369.6 3.7 copy-start.18
  370.8 5.5 copy-start.8
  370.8 5.5 copy-start.11
  373.3 44.5 %copy-start.13 = (f32[128,64]{0,1:T(8,128)S(1)}, f32[128,64]{0,1:T(8,128)}, u32[]{:S(2)}) copy-start(f32[128,64]{0,1:T(8,128)} %copy-done.12) | copy-start | bytes 98308
  376.3 41.7 %copy-start.15 = (f32[128,64]{0,1:T(8,128)S(1)}, f32[128,64]{0,1:T(8,128)}, u32[]{:S(2)}) copy-start(f32[128,64]{0,1:T(8,128)} %copy-done.14) | copy-start | bytes 98308
  459.1 225.1 %reduce-scatter.3.cloned.1.call-start = ((), (), s32[]{:S(2)}) async-start(), calls=%async_computation.4 | async-start | bytes 18898944 | tf_op jit(solution)/shard_map/reduce_scatter | solution.py:312
  502.5 376.8 %all-reduce.9.cloned.1.call-start = ((), (), s32[]{:S(2)}) async-start(), calls=%async_computation.8 | async-start | bytes 18890752
  692.9 190.6 %copy-start.9 = (f32[98368]{0:T(1024)S(1)}, f32[98368]{0:T(1024)}, u32[]{:S(2)}) copy-start(f32[98368]{0:T(1024)} %param.20) | copy-start | bytes 1180420
  692.9 190.6 %copy-start.21 = (f32[98368]{0:T(1024)S(1)}, f32[98368]{0:T(1024)}, u32[]{:S(2)}) copy-start(f32[98368]{0:T(1024)} %param.21) | copy-start | bytes 1180420
  692.9 190.6 %copy-start.22 = (f32[98368]{0:T(1024)S(1)}, f32[98368]{0:T(1024)}, u32[]{:S(2)}) copy-start(f32[98368]{0:T(1024)} %param.22) | copy-start | bytes 1180420
  692.9 191.9 %copy-start.16 = (f32[49152]{0:T(1024)S(1)}, f32[49152]{0:T(1024)}, u32[]{:S(2)}) copy-start(f32[49152]{0:T(1024)} %param.23) | copy-start | bytes 589828
  693.0 191.8 %copy-start.25 = (f32[49152]{0:T(1024)S(1)}, f32[49152]{0:T(1024)}, u32[]{:S(2)}) copy-start(f32[49152]{0:T(1024)} %param.24) | copy-start | bytes 589828
  693.0 191.8 %copy-start.26 = (f32[49152]{0:T(1024)S(1)}, f32[49152]{0:T(1024)}, u32[]{:S(2)}) copy-start(f32[49152]{0:T(1024)} %param.25) | copy-start | bytes 589828
  882.0 3.8 copy-start.10
  (23 other events, 46.4 us)
Sparse Core Ops, SparseCore 0:
  10.8 42.3 all-gather.9
  56.8 102.7 all-reduce.6
  161.2 44.4 all-gather.7
  207.1 80.4 all-gather.5
  459.2 77.1 reduce-scatter.4
  538.6 145.5 reduce-scatter.2
  693.1 186.1 all-reduce.8
where the time goes:
time: 903 us; the launch traced here: 893 us
  waiting for transfers between devices  604 us (67%)
  local copies, waits for them, and re-layouts  157 us (17%)
  matrix products  78.2 us (9%)
  other arithmetic  36.8 us (4%)
  between operations  15.9 us (2%)
    unnamed x9, waiting for transfers between devices  288 us
    reduce_scatter x1, waiting for transfers between devices, per_device(): lax.psum_scatter(attn_cube, 'grp', scatter_dimension=1, tiled=True)  141 us
    all_gather x1, waiting for transfers between devices, per_device(): lax.all_gather(attn_part, 'grp', axis=1, tiled=True)  67 us
    all_gather x1, waiting for transfers between devices, per_device(): lax.all_gather(expert_cube, 'rep', axis=0, tiled=True)  37.1 us
    all_gather x1, waiting for transfers between devices, per_device(): lax.all_gather(expert_part, 'grp', axis=1, tiled=True)  36.8 us
    reduce_scatter x1, waiting for transfers between devices, per_device(): lax.psum_scatter(expert_cube, 'grp', scatter_dimension=1, tiled=True)  33.6 us
    reshape x2, local copies, waits for them, and re-layouts, per_device(): attn_cube = attn_grad_full.reshape(rep_count, grp_count, -1)  29.5 us
    unnamed x105, local copies, waits for them, and re-layouts  27.8 us
  transfers between devices with their start and end apart: 7, of which 7 were waited for; matrix products, arithmetic and copies ran while one was open for 9% of the time, Pallas kernels for 0%

commit v1 on v0

--- a/solution.py
+++ b/solution.py
@@ -21,6 +21,18 @@
 BETA_TWO = 0.95
 ADAM_EPS = 1e-08
 DECAY = 0.1
+
+
+def doubled_up(value, axis, dim):
+    ways, here = (lax.axis_size(axis), lax.axis_index(axis))
+    grown, reach = (value, 1)
+    while reach < ways:
+        theirs = lax.ppermute(grown, axis, [(d, d ^ reach) for d in range(ways)])
+        mine_first = jnp.concatenate([grown, theirs], axis=dim)
+        theirs_first = jnp.concatenate([theirs, grown], axis=dim)
+        grown = jnp.where(here & reach == 0, mine_first, theirs_first)
+        reach = 2 * reach
+    return grown
 
 
 def unpack_attention(flat_vec):
@@ -170,7 +182,7 @@
         lax.all_gather(expert_cube, "rep", axis=0, tiled=True),
     )
     attn_whole, expert_whole = (
-        lax.all_gather(attn_part, "grp", axis=1, tiled=True),
+        doubled_up(attn_part, "grp", 1),
         lax.all_gather(expert_part, "grp", axis=1, tiled=True),
     )
     attn_full = attn_whole.reshape(-1)

time: 903 us -> 821 us (0.909)
  waiting for transfers between devices: 604 us -> 540 us
  matrix products: 78.2 us -> 56 us
    all_gather x1 -> x0, waiting for transfers between devices: 67 us -> none  [per_device(): lax.all_gather(attn_part, 'grp', axis=1, tiled=True)]
    ppermute x0 -> x1, waiting for transfers between devices: none -> 41 us  [doubled_up(): theirs = lax.ppermute(grown, axis, [(d, d ^ reach) for d in range(ways)])]
    all_gather x1, waiting for transfers between devices: 36.8 us -> 0.01 us  [per_device(): lax.all_gather(expert_part, 'grp', axis=1, tiled=True)]
    select_n x0 -> x3, local copies, waits for them, and re-layouts: none -> 35.3 us  [doubled_up(): grown = jnp.where(here & reach == 0, mine_first, theirs_first)]
    slice x2 -> x0, local copies, waits for them, and re-layouts: 20.8 us -> none  [the longest x1 10.4 us: unpack_attention(): flat_vec[start_out:].reshape(QUERY_HEADS * HEAD_SIZE, MODEL_WIDTH)]
    dot_general x8, matrix products: 11.8 us -> 1.23 us  [head_forward(): jnp.einsum('gts,sd->tgd', probs_low, value_low, preferred_element_type=jn...]
    all_gather x1 -> x0, local copies, waits for them, and re-layouts: 10.3 us -> none  [per_device(): lax.all_gather(attn_part, 'grp', axis=1, tiled=True)]
    unnamed x9 -> x8, waiting for transfers between devices: 288 us -> 292 us
  transfers between devices with their start and end apart: 7 -> 7, of which waited for: 7 -> 6; matrix products, arithmetic and copies ran while one was open for 9% -> 15% of each run, Pallas kernels for 0% -> 0%
where the time goes in v1:
time: 821 us; the launch traced here: 814 us
  waiting for transfers between devices  540 us (66%)
  local copies, waits for them, and re-layouts  158 us (19%)
  matrix products  56 us (7%)
  other arithmetic  40.9 us (5%)
  between operations  16.1 us (2%)
    unnamed x8, waiting for transfers between devices  292 us
    reduce_scatter x1, waiting for transfers between devices, per_device(): lax.psum_scatter(attn_cube, 'grp', scatter_dimension=1, tiled=True)  141 us
    ppermute x1, waiting for transfers between devices, doubled_up(): theirs = lax.ppermute(grown, axis, [(d, d ^ reach) for d in range(ways)])  41 us
    select_n x3, local copies, waits for them, and re-layouts, doubled_up(): grown = jnp.where(here & reach == 0, mine_first, theirs_first)  35.3 us
    all_gather x1, waiting for transfers between devices, per_device(): lax.all_gather(expert_cube, 'rep', axis=0, tiled=True)  33.6 us
    reduce_scatter x1, waiting for transfers between devices, per_device(): lax.psum_scatter(expert_cube, 'grp', scatter_dimension=1, tiled=True)  32.8 us
    reshape x2, local copies, waits for them, and re-layouts, per_device(): attn_cube = attn_grad_full.reshape(rep_count, grp_count, -1)  29.5 us
    unnamed x105, local copies, waits for them, and re-layouts  27.3 us
  transfers between devices with their start and end apart: 7, of which 6 were waited for; matrix products, arithmetic and copies ran while one was open for 15% of the time, Pallas kernels for 0%

profile of v1, /device:TPU:0, one launch (start us, length us, event | category | flops | bytes accessed | tf_op | source)
XLA Modules:
  0.0 813.8 jit_solution(7725870854086746890)
XLA Ops:
  14.4 106.9 %all-reduce.7.cloned.1.call-done = bf16[1573888]{0:T(1024)(128)(2,1)} async-done(((bf16[1573888]{0:T(1024)(128)(2,1)}), bf16[1573888]{0:T(1024)(128)(2,1)}) %all-reduce.7.cloned.1.call-update) | async-done | bytes 3147792
  121.3 4.3 reshape.388
  133.5 33.6 %all-gather.7.cloned.1.call-done = bf16[786432]{0:T(1024)(128)(2,1)} async-done(((bf16[49152]{0:T(1024)(128)(2,1)}), bf16[786432]{0:T(1024)(128)(2,1)}) %all-gather.7.cloned.1.call-update) | async-done | bytes 1572880 | tf_op jit(solution)/shard_map/all_gather | solution.py:182
  167.1 2.7 reshape.389
  170.4 41.0 %collective-permute-done = bf16[16,1,98368]{2,0,1:T(8,128)(2,1)} collective-permute-done((bf16[16,1,98368]{2,0,1:T(8,128)(2,1)S(1)}, bf16[16,1,98368]{2,0,1:T(8,128)(2,1)}, u32[]{:S(2)}, u32[]{:S(2)}) %collective-permute-start) | collective-permute-done | bytes 3147808 | tf_op jit(solution)/shard_map/ppermute | solution.py:30
  211.4 5.7 maximum_select_fusion
  217.1 14.2 %copy.79 = bf16[16,2,98368]{2,1,0:T(2,128)(2,1)} copy(bf16[16,2,98368]{2,0,1:T(8,128)(2,1)S(1)} %maximum_select_fusion) | data formatting | bytes 12591104 | tf_op jit(solution)/shard_map/jit(_where)/select_n | solution.py:33
  231.3 8.1 reshape.411
  239.4 10.4 %select_n.54 = bf16[1537,2048]{1,0:T(8,128)(2,1)} reshape(bf16[3147776]{0:T(1024)(128)(2,1)} %reshape.411) | data formatting | bytes 12591104 | tf_op jit(solution)/shard_map/jit(_where)/select_n | solution.py:33
  250.5 3.6 fusion.48
  255.1 8.3 %while.26 = (s32[]{:T(128)}, bf16[8,128,2,64]{1,3,2,0:T(8,128)(2,1)S(1)}, f32[8,2,128,1]{2,1,3,0:T(2,128)}, bf16[8,128,64]{1,2,0:T(8,128)(2,1)S(1)}, bf16[8,128,...) while((s32[]{:T(128)}, bf16[8,128,2,64]{1,3,2,0:T(8,128)(2,1)S(1)}, ...), condition=%wide.region_4.5_spmd, body=%wide.region_1.4_spmd.sunk | while | flops 8650498 | bytes 534617 | solution.py:219
  263.5 10.6 %select_n.55 = bf16[3074,1024]{1,0:T(8,128)(2,1)} reshape(bf16[3147776]{0:T(1024)(128)(2,1)} %reshape.411) | data formatting | bytes 12591104 | tf_op jit(solution)/shard_map/jit(_where)/select_n | solution.py:33
  278.3 5.1 copy.87
  283.4 4.6 slice.81
  288.0 4.8 slice.85
  306.2 2.8 convolution_bitcast_fusion.6
  309.2 30.6 %while.27 = (s32[]{:T(128)}, f32[8,128,2,64]{1,3,2,0:T(8,128)S(1)}, f32[8,128,64]{1,2,0:T(8,128)S(1)}, bf16[8,128,64]{1,2,0:T(8,128)(2,1)S(1)}, bf16[8,128,64]{1...) while((s32[]{:T(128)}, f32[8,128,2,64]{1,3,2,0:T(8,128)S(1)}, ...), condition=%wide.region_12.14_spmd, body=%wide.region_10.13_spmd.sunk | while | flops 21315328 | bytes 1009789 | solution.py:284
  340.5 3.9 fusion.80
  348.1 3.0 copy.99
  351.1 5.2 copy.98
  357.8 4.8 pad_maximum_fusion.1
  362.6 9.2 %reshape.368 = f32[16,2,49152]{2,1,0:T(2,128)} reshape(f32[1572864]{0:T(1024)} %pad_maximum_fusion.1) | data formatting | bytes 12582912 | tf_op jit(solution)/shard_map/reshape | solution.py:322
  371.8 9.1 %copy.92 = f32[16,2,49152]{2,0,1:T(8,128)} copy(f32[16,2,49152]{2,1,0:T(2,128)} %reshape.368) | data formatting | bytes 12582912 | tf_op jit(solution)/shard_map/reshape | solution.py:322
  381.1 13.6 %pad_maximum_fusion = f32[3147776]{0:T(1024)} fusion(f32[1048576]{0:T(1024)} %bitcast.220, f32[2097152]{0:T(1024)} %bitcast.218, f32[1024]{0:T(1024)S(1)} %get-tuple-element.103, f32[1024]{0:T(1024)S(1)} %get-tuple-element.105), kind=kLoop, calls=%fused_computation.63 | loop fusion | flops 9443328 | bytes 25182208 | tf_op jit(solution)/shard_map/concatenate | solution.py:318
  394.7 19.2 %reshape.364 = f32[16,2,98368]{2,1,0:T(2,128)} reshape(f32[3147776]{0:T(1024)} %pad_maximum_fusion) | data formatting | bytes 25182208 | tf_op jit(solution)/shard_map/reshape | solution.py:321
  413.9 10.3 %copy.90 = f32[16,2,98368]{2,0,1:T(8,128)} copy(f32[16,2,98368]{2,1,0:T(2,128)} %reshape.364) | data formatting | bytes 25182208 | tf_op jit(solution)/shard_map/reshape | solution.py:321
  424.5 32.8 %reduce-scatter.5.cloned.1.call-done = f32[16,1,49152]{2,0,1:T(8,128)} async-done(((f32[16,2,49152]{2,0,1:T(8,128)}), f32[16,1,49152]{2,0,1:T(8,128)}) %reduce-scatter.5.cloned.1.call-update) | async-done | bytes 3145744 | tf_op jit(solution)/shard_map/reduce_scatter | solution.py:325
  457.3 6.8 copy.93
  464.1 141.0 %reduce-scatter.3.cloned.1.call-done = f32[16,1,98368]{2,0,1:T(8,128)} async-done(((f32[16,2,98368]{2,0,1:T(8,128)}), f32[16,1,98368]{2,0,1:T(8,128)}) %reduce-scatter.3.cloned.1.call-update) | async-done | bytes 6295568 | tf_op jit(solution)/shard_map/reduce_scatter | solution.py:324
  605.1 8.7 %copy.91 = f32[16,1,98368]{2,1,0:T(1,128)} copy(f32[16,1,98368]{2,0,1:T(8,128)} %reduce-scatter.3.cloned.1.call-done) | data formatting | bytes 12591104 | tf_op jit(solution)/shard_map/reduce_scatter | solution.py:324
  615.5 184.7 %all-reduce.9.cloned.1.call-done = (f32[16,1,98368]{2,1,0:T(1,128)}, f32[16,1,49152]{2,1,0:T(1,128)}) async-done(((f32[16,1,98368]{2,1,0:T(1,128)}, f32[16,1,49152]{2,1,0:T(1,128)}), (f32[16,1,98368]{2,1,0:T(1,128)}, f32[16,1,49152]{2,1,0:T(1,128)})) %all-reduce.9.cloned.1.call-update) | async-done | bytes 9441296
  800.2 2.6 dynamic-slice_reduce_fusion
  (282 shorter events, 83.9 us)
Async XLA Ops:
  7.2 114.1 %all-reduce.7.cloned.1.call-start = ((), (), s32[]{:S(2)}) async-start(), calls=%async_computation.6 | async-start | bytes 6295552
  12.6 116.2 %copy-start.42 = (f32[128,8]{0,1:T(8,128)S(1)}, f32[128,8]{0,1:T(8,128)}, u32[]{:S(2)}) copy-start(f32[128,8]{0,1:T(8,128)} %param.19) | copy-start | bytes 12292
  12.6 116.2 %copy-start.43 = (s32[128,8]{0,1:T(8,128)S(1)}, s32[128,8]{0,1:T(8,128)}, u32[]{:S(2)}) copy-start(s32[128,8]{0,1:T(8,128)} %param.18) | copy-start | bytes 12292
  14.3 116.4 %copy-start.4 = (bf16[128,1024]{1,0:T(8,128)(2,1)S(1)}, bf16[128,1024]{1,0:T(8,128)(2,1)}, u32[]{:S(2)}) copy-start(bf16[128,1024]{1,0:T(8,128)(2,1)} %param.16) | copy-start | bytes 786436
  14.4 152.8 %all-gather.7.cloned.1.call-start = ((), (), s32[]{:S(2)}) async-start(), calls=%async_computation.5 | async-start | bytes 1671168 | tf_op jit(solution)/shard_map/all_gather | solution.py:182
  125.6 85.8 %collective-permute-start = (bf16[16,1,98368]{2,0,1:T(8,128)(2,1)S(1)}, bf16[16,1,98368]{2,0,1:T(8,128)(2,1)}, u32[]{:S(2)}, u32[]{:S(2)}) collective-permute-start(bf16[16,1,98368]{2,0,1:T(8,128)(2,1)S(1)} %reshape.388), channel_id=1, source_target_pairs={{0,1},{1,0},{2,3},{3,2},{4,5},{5,4},{6,7},{7,6},{8,9},{9,8},{10,11... | collective-permute-start | bytes 9443336 | tf_op jit(solution)/shard_map/ppermute | solution.py:30
  128.8 149.5 %all-gather.5.cloned.1.call-start = ((), (), s32[]{:S(2)}) async-start(), calls=%async_computation.2 | async-start | bytes 4718592 | tf_op jit(solution)/shard_map/all_gather | solution.py:186
  128.9 88.2 %copy-start.44 = (f32[128]{0:T(128)}, f32[128]{0:T(128)S(1)}, u32[]{:S(2)}) copy-start(f32[128]{0:T(128)S(1)} %get-tuple-element.152) | copy-start | bytes 1540
  129.9 87.1 %copy-start.38 = (s32[128]{0:T(128)}, s32[128]{0:T(128)S(1)}, u32[]{:S(2)}) copy-start(s32[128]{0:T(128)S(1)} %get-tuple-element.151) | copy-start | bytes 1540
  131.5 119.0 %copy-start.40 = (f32[128]{0:T(128)}, f32[128]{0:T(128)S(1)}, u32[]{:S(2)}) copy-start(f32[128]{0:T(128)S(1)} %get-tuple-element.176) | copy-start | bytes 1540
  169.8 287.5 %reduce-scatter.5.cloned.1.call-start = ((), (), s32[]{:S(2)}) async-start(), calls=%async_computation.4 | async-start | bytes 9437184 | tf_op jit(solution)/shard_map/reduce_scatter | solution.py:325
  263.5 10.7 %copy-start.5 = (bf16[8,128,2,64]{1,3,2,0:T(8,128)(2,1)}, bf16[8,128,2,64]{1,3,2,0:T(8,128)(2,1)S(1)}, u32[]{:S(2)}) copy-start(bf16[8,128,2,64]{1,3,2,0:T(8,128)(2,1)S(1)} %get-tuple-element.370) | copy-start | bytes 786436
  263.5 10.7 %copy-start.20 = (bf16[8,128,64]{1,2,0:T(8,128)(2,1)}, bf16[8,128,64]{1,2,0:T(8,128)(2,1)S(1)}, u32[]{:S(2)}) copy-start(bf16[8,128,64]{1,2,0:T(8,128)(2,1)S(1)} %get-tuple-element.373) | copy-start | bytes 393220
  263.5 10.7 %copy-start.18 = (bf16[8,128,2,64]{1,3,2,0:T(8,128)(2,1)}, bf16[8,128,2,64]{1,3,2,0:T(8,128)(2,1)S(1)}, u32[]{:S(2)}) copy-start(bf16[8,128,2,64]{1,3,2,0:T(8,128)(2,1)S(1)} %get-tuple-element.321) | copy-start | bytes 786436
  277.2 10.8 %copy-start.34 = (f32[128]{0:T(128)}, f32[128]{0:T(128)S(1)}, u32[]{:S(2)}) copy-start(f32[128]{0:T(128)S(1)} %get-tuple-element.178) | copy-start | bytes 1540
  294.9 5.0 copy-start.35
  296.7 5.1 copy-start.28
  296.7 5.1 copy-start.30
  296.7 5.1 copy-start.32
  303.7 5.5 copy-start.7
  303.7 5.5 copy-start.10
  303.7 5.5 copy-start.27
  306.2 33.7 %copy-start.12 = (f32[128,64]{0,1:T(8,128)S(1)}, f32[128,64]{0,1:T(8,128)}, u32[]{:S(2)}) copy-start(f32[128,64]{0,1:T(8,128)} %get-tuple-element.184) | copy-start | bytes 98308
  309.2 30.9 %copy-start.14 = (f32[128,64]{0,1:T(8,128)S(1)}, f32[128,64]{0,1:T(8,128)}, u32[]{:S(2)}) copy-start(f32[128,64]{0,1:T(8,128)} %get-tuple-element.183) | copy-start | bytes 98308
  381.0 224.1 %reduce-scatter.3.cloned.1.call-start = ((), (), s32[]{:S(2)}) async-start(), calls=%async_computation.3 | async-start | bytes 18898944 | tf_op jit(solution)/shard_map/reduce_scatter | solution.py:324
  424.2 375.9 %all-reduce.9.cloned.1.call-start = ((), (), s32[]{:S(2)}) async-start(), calls=%async_computation.7 | async-start | bytes 18890752
  613.8 190.6 %copy-start.8 = (f32[98368]{0:T(1024)S(1)}, f32[98368]{0:T(1024)}, u32[]{:S(2)}) copy-start(f32[98368]{0:T(1024)} %param.20) | copy-start | bytes 1180420
  613.8 190.6 %copy-start.22 = (f32[98368]{0:T(1024)S(1)}, f32[98368]{0:T(1024)}, u32[]{:S(2)}) copy-start(f32[98368]{0:T(1024)} %param.21) | copy-start | bytes 1180420
  613.8 190.6 %copy-start.23 = (f32[98368]{0:T(1024)S(1)}, f32[98368]{0:T(1024)}, u32[]{:S(2)}) copy-start(f32[98368]{0:T(1024)} %param.22) | copy-start | bytes 1180420
  613.8 191.8 %copy-start.15 = (f32[49152]{0:T(1024)S(1)}, f32[49152]{0:T(1024)}, u32[]{:S(2)}) copy-start(f32[49152]{0:T(1024)} %param.23) | copy-start | bytes 589828
  613.8 191.8 %copy-start.25 = (f32[49152]{0:T(1024)S(1)}, f32[49152]{0:T(1024)}, u32[]{:S(2)}) copy-start(f32[49152]{0:T(1024)} %param.24) | copy-start | bytes 589828
  613.9 191.8 %copy-start.26 = (f32[49152]{0:T(1024)S(1)}, f32[49152]{0:T(1024)}, u32[]{:S(2)}) copy-start(f32[49152]{0:T(1024)} %param.25) | copy-start | bytes 589828
  (23 other events, 53.2 us)
Sparse Core Ops, SparseCore 0:
  14.5 106.7 all-reduce.6
  128.9 38.2 all-gather.6
  170.0 58.1 all-gather.4
  381.1 76.1 reduce-scatter.4
  459.5 145.5 reduce-scatter.2
  613.9 186.1 all-reduce.8
